TPU v7x, 256 devices: a whole 4x4x8 slice. The times are simulated.
256 devices in a mesh: req: 4 (over y), blk: 16 (over z, x_lo), tp: 4 (over x_hi, core).
Axes of the slice: x: 4 (x_hi: 2, x_lo: 2; x = x_hi * 2 + x_lo), y: 4, z: 8, core: 2. Of those that a mesh axis runs over, the one named last changes fastest.
Arguments:
- tokens: bfloat16 [4, 2048, 5120], P('req', 'blk', 'tp'), may hold values from -6 to 6
- gain: bfloat16 [5120], replicated, may hold values from 0.5 to 1.5
- w_query: bfloat16 [5120, 5120], P('req', 'tp'), may hold values from -0.078125 to 0.078125
- b_query: bfloat16 [5120], P('tp'), may hold values from -4 to 4
- w_keyval: bfloat16 [5120, 2, 1024], P('req', None, 'tp'), may hold values from -0.078125 to 0.078125
- b_keyval: bfloat16 [2, 1024], P(None, 'tp'), may hold values from -3 to 3
- kv_cache: bfloat16 [4, 2, 112, 128, 1024], P('req', None, 'blk', None, 'tp'), may hold values from -400 to 400
- cached_pages: int32 [4], P('req'), may hold values from 1 to 64, as said below
- page_table: int32 [4, 80], P('req'), may hold values from -1 to 111, as said below
Outputs:
- attended: bfloat16 [4, 2048, 5120], P('req', 'blk', 'tp')
- new_cache: bfloat16 [4, 2, 112, 128, 1024], P('req', None, 'blk', None, 'tp')
Inputs may be any that keep to these rules, and one draw needn't show every extreme that they name: `cached_pages`: one request has the most, 64. `page_table`: entry p of a request's row is the slot (owner index of blk times 7 plus slot) of its logical page p for p below its cached pages plus 16, and -1 beyond; the live pages of a request use distinct slots; one index of blk holds at most 4 cached pages of a request; the request with 64 cached pages has exactly 4 on every index of blk.
All inputs are finite; a program needn't handle non-finite values.
Results may differ from a plain program's by a relative error of at most 0.012.
The roundings to bfloat16 on the way count: a program that leaves them out, or rounds other values in their place, can miss the bound.
Values may be sent and summed in bfloat16 or wider, within the bound.
A program may use at most 128 MiB of HBM per device.

v0:
```python
import jax
import jax.numpy as jnp
from jax import lax
from jax.sharding import PartitionSpec as P

HEAD_SIZE = 128
PAGE_TOKENS = 128
epsilon = 1e-06
rope_base = 1000000.0


def normalize(inputs, gain):
    floats = inputs.astype(jnp.float32)
    scaling = lax.rsqrt(jnp.mean(floats * floats, axis=-1, keepdims=True) + epsilon)
    return (floats * scaling * gain.astype(jnp.float32)).astype(jnp.bfloat16)


def apply_rotation(vectors, token_positions):
    halfway = vectors.shape[-1] // 2
    frequency = rope_base ** (-(jnp.arange(halfway, dtype=jnp.float32) * 2.0 / vectors.shape[-1]))
    angles = token_positions[:, None] * frequency[None, :]
    cosine = jnp.cos(angles)[:, None, :]
    sine_part = jnp.sin(angles)[:, None, :]
    leading = vectors[..., :halfway]
    trailing = vectors[..., halfway:]
    return jnp.concatenate(
        [leading * cosine - trailing * sine_part, trailing * cosine + leading * sine_part], axis=-1
    )


def attend(running, query_rows_all, key_rows, value_rows, allowed):
    scaling = HEAD_SIZE ** (-0.5)
    scores = (
        jnp.einsum("rgjd,kgd->rgjk", query_rows_all, key_rows, preferred_element_type=jnp.float32)
        * scaling
    )
    scores = jnp.where(allowed[:, None, None, :], scores, -jnp.inf)
    maxima, totals, blended = running
    fresh_max = jnp.maximum(maxima, jnp.max(scores, axis=-1))
    weights = jnp.exp(scores - fresh_max[..., None])
    decays = jnp.exp(maxima - fresh_max)
    totals = totals * decays + jnp.sum(weights, axis=-1)
    blended = blended * decays[..., None] + jnp.einsum(
        "rgjk,kgd->rgjd",
        weights.astype(jnp.bfloat16),
        value_rows,
        preferred_element_type=jnp.float32,
    )
    return (fresh_max, totals, blended)


def make_fold(usable_all, query_rows_all, kv_heads_local, running, pieces):
    count = pieces.shape[1]
    stride = max((divisor for divisor in (4, 3, 2, 1) if count % divisor == 0))

    def advance(counter, carried):
        segment = lax.dynamic_slice_in_dim(pieces, counter * stride, stride, 1)
        usable = lax.dynamic_slice_in_dim(usable_all, counter * stride, stride)
        key_rows = segment[0].reshape(stride * PAGE_TOKENS, kv_heads_local, HEAD_SIZE)
        value_rows = segment[1].reshape(stride * PAGE_TOKENS, kv_heads_local, HEAD_SIZE)
        allowed = jnp.repeat(usable, PAGE_TOKENS)[None, :]
        return attend(carried, query_rows_all, key_rows, value_rows, allowed)

    return lax.fori_loop(0, count // stride, advance, running)


def body(tokens, gain, w_query, b_query, w_keyval, b_keyval, kv_cache, cached_pages, page_table):
    whole = lax.all_gather(tokens[0], "tp", axis=1, tiled=True)
    normed = normalize(whole, gain)
    rows_here = normed.shape[0]
    query_width = w_query.shape[1]
    kv_width = w_keyval.shape[2]
    pair_width = 2 * kv_width
    pieces = (
        lax.all_gather(w_query, "req", axis=0, tiled=True),
        lax.all_gather(w_keyval, "req", axis=0, tiled=True),
    )
    count = pieces[0].shape[0]
    query_sum = jnp.dot(normed, pieces[0], preferred_element_type=jnp.float32)
    pair_sum = jnp.dot(
        normed, pieces[1].reshape(count, pair_width), preferred_element_type=jnp.float32
    )
    length = cached_pages[0]
    page_map = page_table[0]
    own_index = lax.axis_index("blk")
    cycle_size = lax.axis_size("blk")
    heads_local = query_width // HEAD_SIZE
    kv_heads_local = kv_width // HEAD_SIZE
    queries_per_group = heads_local // kv_heads_local
    token_index = own_index * rows_here + jnp.arange(rows_here, dtype=jnp.int32)
    token_positions = (length * PAGE_TOKENS + token_index).astype(jnp.float32)
    query_full = query_sum + b_query.astype(jnp.float32)
    query_rows_all = apply_rotation(
        query_full.reshape(rows_here, heads_local, HEAD_SIZE), token_positions
    ).astype(jnp.bfloat16)
    query_rows_all = query_rows_all.reshape(rows_here, kv_heads_local, queries_per_group, HEAD_SIZE)
    pair_full = pair_sum + b_keyval.reshape(pair_width).astype(jnp.float32)
    fresh_key = apply_rotation(
        pair_full[:, :kv_width].reshape(rows_here, kv_heads_local, HEAD_SIZE), token_positions
    ).astype(jnp.bfloat16)
    fresh_value = pair_full[:, kv_width:].astype(jnp.bfloat16)
    fresh_pages = jnp.stack([fresh_key.reshape(rows_here, kv_width), fresh_value]).reshape(
        2, rows_here // PAGE_TOKENS, PAGE_TOKENS, kv_width
    )
    every_page = lax.all_gather(fresh_pages, "blk", axis=1, tiled=True)
    new_count = every_page.shape[1]
    fresh_rows = new_count * PAGE_TOKENS
    new_keys = every_page[0].reshape(fresh_rows, kv_heads_local, HEAD_SIZE)
    new_values = every_page[1].reshape(fresh_rows, kv_heads_local, HEAD_SIZE)
    allowed_fresh = jnp.arange(fresh_rows, dtype=jnp.int32)[None, :] <= token_index[:, None]
    starting = (
        jnp.full((rows_here, kv_heads_local, queries_per_group), -jnp.inf, jnp.float32),
        jnp.zeros((rows_here, kv_heads_local, queries_per_group), jnp.float32),
        jnp.zeros((rows_here, kv_heads_local, queries_per_group, HEAD_SIZE), jnp.float32),
    )
    running = attend(starting, query_rows_all, new_keys, new_values, allowed_fresh)
    cache_storage = kv_cache[0]
    slot_count = cache_storage.shape[1]
    new_slots = lax.dynamic_slice_in_dim(page_map, length, new_count)
    chooser = (
        new_slots[None, :]
        == own_index * slot_count + jnp.arange(slot_count, dtype=jnp.int32)[:, None]
    )
    written = jnp.einsum(
        "sj,cjpw->cspw",
        chooser.astype(jnp.bfloat16),
        every_page,
        preferred_element_type=jnp.float32,
    ).astype(jnp.bfloat16)
    landed = jnp.any(chooser, axis=1)
    new_storage = jnp.where(landed[None, :, None, None], written, cache_storage)
    pool_size = cycle_size * slot_count
    live = jnp.arange(page_map.shape[0], dtype=jnp.int32) < length
    matches = (page_map[None, :] == jnp.arange(pool_size, dtype=jnp.int32)[:, None]) & live[None, :]
    valid = jnp.any(matches, axis=1)
    running = make_fold(
        valid,
        query_rows_all,
        kv_heads_local,
        running,
        lax.all_gather(cache_storage, "blk", axis=1, tiled=True),
    )
    maxima, totals, blended = running
    result = (blended / totals[..., None]).reshape(rows_here, query_width).astype(jnp.bfloat16)
    return (result[None], new_storage[None])


def solution(mesh):
    return jax.shard_map(
        body,
        mesh=mesh,
        in_specs=(
            P("req", "blk", "tp"),
            P(),
            P("req", "tp"),
            P("tp"),
            P("req", None, "tp"),
            P(None, "tp"),
            P("req", None, "blk", None, "tp"),
            P("req"),
            P("req", None),
        ),
        out_specs=(P("req", "blk", "tp"), P("req", None, "blk", None, "tp")),
        check_vma=False,
    )
```

profile of v0, /device:TPU:35, one launch (start us, length us, event | category | flops | bytes accessed | tf_op | source)
XLA Modules:
  0.0 774.0 jit_solution(6554469855381495535)
XLA Ops:
  11.2 25.5 %all-gather.13.cloned.1.call-done = bf16[1,128,5120]{2,1,0:T(8,128)(2,1)} async-done(((bf16[1,128,1280]{2,1,0:T(8,128)(2,1)}), bf16[1,128,5120]{2,1,0:T(8,128)(2,1)}) %all-gather.13.cloned.1.call-update) | async-done | bytes 1310736 | tf_op jit(solution)/shard_map/all_gather | solution.py:68
  38.4 59.7 %all-gather.9.cloned.1.call-done = bf16[5120,2,256]{2,1,0:T(2,128)(2,1)} async-done(((bf16[1280,2,256]{2,1,0:T(2,128)(2,1)}), bf16[5120,2,256]{2,1,0:T(2,128)(2,1)}) %all-gather.9.cloned.1.call-update) | async-done | bytes 5242896 | tf_op jit(solution)/shard_map/all_gather | solution.py:76
  98.1 3.5 copy.82
  106.3 60.9 %all-gather.15.cloned.1.call-done = bf16[2,2048,256]{2,1,0:T(8,128)(2,1)} async-done(((bf16[2,128,256]{2,1,0:T(8,128)(2,1)}), bf16[2,2048,256]{2,1,0:T(8,128)(2,1)}) %all-gather.15.cloned.1.call-update) | async-done | bytes 2097168 | tf_op jit(solution)/shard_map/all_gather | solution.py:105
  170.7 3.5 fusion.40
  175.3 127.5 %all-gather.11.cloned.1.call-done = bf16[5120,1280]{1,0:T(8,128)(2,1)} async-done(((bf16[1280,1280]{1,0:T(8,128)(2,1)}), bf16[5120,1280]{1,0:T(8,128)(2,1)}) %all-gather.11.cloned.1.call-update) | async-done | bytes 13107216 | tf_op jit(solution)/shard_map/all_gather | solution.py:75
  302.8 6.6 convolution_add_fusion
  315.9 3.6 fusion.46
  319.4 299.3 %all-gather.17.cloned.1.call-done = bf16[1,2,112,128,256]{4,3,2,1,0:T(8,128)(2,1)} async-done(((bf16[1,2,7,128,256]{4,3,2,1,0:T(8,128)(2,1)}), bf16[1,2,112,128,256]{4,3,2,1,0:T(8,128)(2,1)}) %all-gather.17.cloned.1.call-update) | async-done | bytes 14680080 | tf_op jit(solution)/shard_map/all_gather | solution.py:141
  618.7 146.7 %while.17 = (s32[]{:T(128)}, f32[128,2,5]{0,2,1:T(8,128)S(1)}, f32[128,2,5]{0,2,1:T(8,128)S(1)}, f32[128,2,5,128]{0,3,2,1:T(8,128)}, pred[112]{0:T(512)(128)(4,1...) while((s32[]{:T(128)}, f32[128,2,5]{0,2,1:T(8,128)S(1)}, ...), condition=%wide.region_7.8_spmd, body=%wide.region_4.0_spmd.sunk | while | flops 343083520 | bytes 12208327 | solution.py:64
  626.5 2.7 fusion.76
  636.9 2.7 fusion.76
  647.4 2.7 fusion.76
  657.9 2.7 fusion.76
  668.4 2.7 fusion.76
  678.9 2.7 fusion.76
  689.3 2.7 fusion.76
  699.8 2.7 fusion.76
  710.3 2.7 fusion.76
  720.8 2.7 fusion.76
  731.2 2.7 fusion.76
  741.7 2.7 fusion.76
  752.2 2.7 fusion.76
  762.7 2.7 fusion.76
  (353 shorter events, 130.0 us)
Async XLA Ops:
  7.2 29.5 %all-gather.13.cloned.1.call-start = ((), (), s32[]{:S(2)}) async-start(), calls=%async_computation.2 | async-start | bytes 1638400 | tf_op jit(solution)/shard_map/all_gather | solution.py:68
  7.9 90.2 %all-gather.9.cloned.1.call-start = ((), (), s32[]{:S(2)}) async-start(), calls=%async_computation | async-start | bytes 6553600 | tf_op jit(solution)/shard_map/all_gather | solution.py:76
  8.6 158.6 %all-gather.15.cloned.1.call-start = ((), (), s32[]{:S(2)}) async-start(), calls=%async_computation.3 | async-start | bytes 2228224 | tf_op jit(solution)/shard_map/all_gather | solution.py:105
  98.1 3.5 copy-start
  102.6 2.4 copy-start.3
  102.6 2.5 copy-start.4
  103.8 199.0 %all-gather.11.cloned.1.call-start = ((), (), s32[]{:S(2)}) async-start(), calls=%async_computation.1 | async-start | bytes 16384000 | tf_op jit(solution)/shard_map/all_gather | solution.py:75
  104.4 514.3 %all-gather.17.cloned.1.call-start = ((), (), s32[]{:S(2)}) async-start(), calls=%async_computation.4 | async-start | bytes 15597568 | tf_op jit(solution)/shard_map/all_gather | solution.py:141
  309.5 2.6 copy-start.2
  309.7 2.4 copy-start.1
Sparse Core Ops, SparseCore 0:
  9.8 26.8 all-gather.12
  38.5 59.5 all-gather.8
  104.0 63.2 all-gather.14
  168.9 133.8 all-gather.10
  304.5 314.2 all-gather.16
where the time goes:
time: 776 us; the launch traced here: 774 us
  waiting for transfers between devices  575 us (74%)
  matrix products  107 us (14%)
  local copies, waits for them, and re-layouts  48.8 us (6%)
  other arithmetic  26.9 us (3%)
  between operations  14.7 us (2%)
    all_gather x1, waiting for transfers between devices, body(): lax.all_gather(cache_storage, 'blk', axis=1, tiled=True)  299 us
    all_gather x1, waiting for transfers between devices, body(): lax.all_gather(w_query, 'req', axis=0, tiled=True)  127 us
    dot_general x29, matrix products, attend(): jnp.einsum('rgjk,kgd->rgjd', weights.astype(jnp.bfloat16), value_rows, pr...  79.7 us
    all_gather x1, waiting for transfers between devices, body(): every_page = lax.all_gather(fresh_pages, 'blk', axis=1, tiled=True)  60.9 us
    all_gather x1, waiting for transfers between devices, body(): lax.all_gather(w_keyval, 'req', axis=0, tiled=True)  59.7 us
    slice x28, local copies, waits for them, and re-layouts, advance(): segment[1].reshape(stride * PAGE_TOKENS, kv_heads_local, HEAD_SIZE)  29.8 us
    all_gather x1, waiting for transfers between devices, body(): whole = lax.all_gather(tokens[0], 'tp', axis=1, tiled=True)  25.5 us
    reduce_sum x29, other arithmetic, attend(): totals = totals * decays + jnp.sum(weights, axis=-1)  18.7 us
  transfers between devices with their start and end apart: 5, of which 5 were waited for; matrix products, arithmetic and copies ran while one was open for 4% of the time, Pallas kernels for 0%

commit v1 on v0

--- a/solution.py
+++ b/solution.py
@@ -1,3 +1,4 @@
+import functools
 import jax
 import jax.numpy as jnp
 from jax import lax
@@ -7,6 +8,31 @@
 PAGE_TOKENS = 128
 epsilon = 1e-06
 rope_base = 1000000.0
+
+
+def enter_the_terms(page, axis_key, axis_no):
+    formed = jax.lax.axis_size(axis_key)
+    q_next, response, oldest = (formed, jax.lax.axis_index(axis_key), page.shape[axis_no])
+    slots = [tick * q_next if p == axis_no else tick for p, tick in enumerate(page.shape)]
+    inter = jnp.zeros(slots, page.dtype)
+    new = lax.dynamic_update_slice_in_dim(inter, page, response * oldest, axis=axis_no)
+    newest = finding = page
+    for q in [*range(1, q_next // 2 + 1)]:
+        newest = jax.lax.ppermute(newest, axis_key, [(p, (p + 1) % q_next) for p in range(q_next)])
+        new = lax.dynamic_update_slice_in_dim(
+            new, newest, (response - q) % q_next * oldest, axis=axis_no
+        )
+        if 2 * q < q_next:
+            finding = jax.lax.ppermute(
+                finding, axis_key, [(p, (p - 1) % q_next) for p in range(q_next)]
+            )
+            new = lax.dynamic_update_slice_in_dim(
+                new, finding, (response + q) % q_next * oldest, axis=axis_no
+            )
+    return new
+
+
+rails_review = functools.partial(enter_the_terms, axis_key="req", axis_no=0)
 
 
 def normalize(inputs, gain):
@@ -71,10 +97,7 @@
     query_width = w_query.shape[1]
     kv_width = w_keyval.shape[2]
     pair_width = 2 * kv_width
-    pieces = (
-        lax.all_gather(w_query, "req", axis=0, tiled=True),
-        lax.all_gather(w_keyval, "req", axis=0, tiled=True),
-    )
+    pieces = (rails_review(w_query), lax.all_gather(w_keyval, "req", axis=0, tiled=True))
     count = pieces[0].shape[0]
     query_sum = jnp.dot(normed, pieces[0], preferred_element_type=jnp.float32)
     pair_sum = jnp.dot(

time: 776 us -> 648 us (0.84)
  waiting for transfers between devices: 575 us -> 425 us
  local copies, waits for them, and re-layouts: 48.8 us -> 68.5 us
    all_gather x1 -> x0, waiting for transfers between devices: 127 us -> none  [body(): lax.all_gather(w_query, 'req', axis=0, tiled=True)]
    ppermute x0 -> x3, waiting for transfers between devices: none -> 124 us  [the longest x2 124 us: enter_the_terms(): jax.lax.ppermute(newest, axis_key, [(p, (p + 1) % q_next) for p in range(...]
    all_gather x1, waiting for transfers between devices: 299 us -> 214 us  [body(): lax.all_gather(cache_storage, 'blk', axis=1, tiled=True)]
    all_gather x1, waiting for transfers between devices: 60.9 us -> 0.02 us  [body(): every_page = lax.all_gather(fresh_pages, 'blk', axis=1, tiled=True)]
    dynamic_update_slice x0 -> x4, local copies, waits for them, and re-layouts: none -> 15.6 us  [the longest x2 7.96 us: enter_the_terms(): lax.dynamic_update_slice_in_dim(new, newest, (response - q) % q_next * ol...]
  transfers between devices with their start and end apart: 5 -> 7, of which waited for: 5 -> 5; matrix products, arithmetic and copies ran while one was open for 4% -> 8% of each run, Pallas kernels for 0% -> 0%
where the time goes in v1:
time: 648 us; the launch traced here: 646 us
  waiting for transfers between devices  425 us (66%)
  matrix products  107 us (17%)
  local copies, waits for them, and re-layouts  68.5 us (11%)
  other arithmetic  26.2 us (4%)
  between operations  14.7 us (2%)
    all_gather x1, waiting for transfers between devices, body(): lax.all_gather(cache_storage, 'blk', axis=1, tiled=True)  214 us
    ppermute x2, waiting for transfers between devices, enter_the_terms(): jax.lax.ppermute(newest, axis_key, [(p, (p + 1) % q_next) for p in range(...  124 us
    dot_general x29, matrix products, attend(): jnp.einsum('rgjk,kgd->rgjd', weights.astype(jnp.bfloat16), value_rows, pr...  79.8 us
    all_gather x1, waiting for transfers between devices, body(): lax.all_gather(w_keyval, 'req', axis=0, tiled=True)  59.7 us
    slice x28, local copies, waits for them, and re-layouts, advance(): segment[1].reshape(stride * PAGE_TOKENS, kv_heads_local, HEAD_SIZE)  29.8 us
    all_gather x1, waiting for transfers between devices, body(): whole = lax.all_gather(tokens[0], 'tp', axis=1, tiled=True)  25.5 us
    reduce_sum x29, other arithmetic, attend(): totals = totals * decays + jnp.sum(weights, axis=-1)  18.7 us
    dot_general x29, matrix products, attend(): jnp.einsum('rgjd,kgd->rgjk', query_rows_all, key_rows, preferred_element_...  16.1 us
  transfers between devices with their start and end apart: 7, of which 5 were waited for; matrix products, arithmetic and copies ran while one was open for 8% of the time, Pallas kernels for 0%

profile of v1, /device:TPU:35, one launch (start us, length us, event | category | flops | bytes accessed | tf_op | source)
XLA Modules:
  0.0 645.7 jit_solution(1142708359110865976)
XLA Ops:
  11.2 25.5 %all-gather.10.cloned.1.call-done = bf16[1,128,5120]{2,1,0:T(8,128)(2,1)} async-done(((bf16[1,128,1280]{2,1,0:T(8,128)(2,1)}), bf16[1,128,5120]{2,1,0:T(8,128)(2,1)}) %all-gather.10.cloned.1.call-update) | async-done | bytes 1310736 | tf_op jit(solution)/shard_map/all_gather | solution.py:94
  38.4 59.7 %all-gather.8.cloned.1.call-done = bf16[5120,2,256]{2,1,0:T(2,128)(2,1)} async-done(((bf16[1280,2,256]{2,1,0:T(2,128)(2,1)}), bf16[5120,2,256]{2,1,0:T(2,128)(2,1)}) %all-gather.8.cloned.1.call-update) | async-done | bytes 5242896 | tf_op jit(solution)/shard_map/all_gather | solution.py:100
  98.1 3.5 copy.82
  107.2 70.6 %collective-permute-done = bf16[1280,1280]{1,0:T(8,128)(2,1)} collective-permute-done((bf16[1280,1280]{1,0:T(8,128)(2,1)}, bf16[1280,1280]{1,0:T(8,128)(2,1)}, u32[]{:S(2)}, u32[]{:S(2)}) %collective-permute-start) | collective-permute-done | bytes 3276832 | tf_op jit(solution)/shard_map/ppermute | solution.py:21
  179.1 5.7 broadcast_in_dim.99
  184.8 3.8 constant_dynamic-update-slice_fusion.3
  188.6 4.1 constant_dynamic-update-slice_fusion.2
  192.7 3.8 constant_dynamic-update-slice_fusion.1
  196.5 53.7 %collective-permute-done.2 = bf16[1280,1280]{1,0:T(8,128)(2,1)} collective-permute-done((bf16[1280,1280]{1,0:T(8,128)(2,1)}, bf16[1280,1280]{1,0:T(8,128)(2,1)}, u32[]{:S(2)}, u32[]{:S(2)}) %collective-permute-start.2) | collective-permute-done | bytes 3276832 | tf_op jit(solution)/shard_map/ppermute | solution.py:21
  250.2 3.8 constant_dynamic-update-slice_fusion
  254.0 6.7 %convolution_add_fusion = f32[128,1280]{1,0:T(8,128)S(1)} fusion(bf16[5120,1280]{1,0:T(8,128)(2,1)} %constant_dynamic-update-slice_fusion, bf16[1,128,5120]{2,1,0:T(8,128)(2,1)S(1)} %copy-done, f32[5120]{0:T(1024)S(1)} %convert_element_type.74, f32[128]{0:T(128)S(1)} %add_rsqrt_fusion, f32[1280]{0:T(1024)S(1)} %convert_element_type.80), kind=kOutput, calls=%fused_computation.35 | convolution fusion | flops 1680506880 | bytes 15099392 | tf_op jit(solution)/shard_map/dot_general | solution.py:102
  264.6 3.5 fusion.40
  273.1 3.6 fusion.46
  276.7 213.7 %all-gather.14.cloned.1.call-done = bf16[1,2,112,128,256]{4,3,2,1,0:T(8,128)(2,1)} async-done(((bf16[1,2,7,128,256]{4,3,2,1,0:T(8,128)(2,1)}), bf16[1,2,112,128,256]{4,3,2,1,0:T(8,128)(2,1)}) %all-gather.14.cloned.1.call-update) | async-done | bytes 14680080 | tf_op jit(solution)/shard_map/all_gather | solution.py:164
  490.4 146.7 %while.17 = (s32[]{:T(128)}, f32[128,2,5]{0,2,1:T(8,128)S(1)}, f32[128,2,5]{0,2,1:T(8,128)S(1)}, f32[128,2,5,128]{0,3,2,1:T(8,128)}, pred[112]{0:T(512)(128)(4,1...) while((s32[]{:T(128)}, f32[128,2,5]{0,2,1:T(8,128)S(1)}, ...), condition=%wide.region_7.8_spmd, body=%wide.region_4.7_spmd.sunk | while | flops 343083520 | bytes 12208327 | solution.py:90
  492.9 2.7 fusion.77
  498.2 2.7 fusion.77
  513.9 2.7 fusion.77
  524.3 2.7 fusion.77
  529.6 2.7 fusion.77
  540.1 2.7 fusion.77
  555.8 2.7 fusion.77
  576.7 2.7 fusion.77
  592.4 2.7 fusion.77
  (359 shorter events, 143.5 us)
Async XLA Ops:
  7.2 29.5 %all-gather.10.cloned.1.call-start = ((), (), s32[]{:S(2)}) async-start(), calls=%async_computation.1 | async-start | bytes 1638400 | tf_op jit(solution)/shard_map/all_gather | solution.py:94
  7.9 90.2 %all-gather.8.cloned.1.call-start = ((), (), s32[]{:S(2)}) async-start(), calls=%async_computation | async-start | bytes 6553600 | tf_op jit(solution)/shard_map/all_gather | solution.py:100
  8.6 253.1 %all-gather.12.cloned.1.call-start = ((), (), s32[]{:S(2)}) async-start(), calls=%async_computation.2 | async-start | bytes 2228224 | tf_op jit(solution)/shard_map/all_gather | solution.py:128
  98.1 3.5 copy-start
  102.5 75.3 %copy-start.2 = (bf16[1280]{0:T(1024)(128)(2,1)S(1)}, bf16[1280]{0:T(1024)(128)(2,1)}, u32[]{:S(2)}) copy-start(bf16[1280]{0:T(1024)(128)(2,1)} %param.14) | copy-start | bytes 7684
  102.5 75.4 %copy-start.3 = (s32[1,80]{1,0:T(1,128)S(1)}, s32[1,80]{1,0:T(1,128)}, u32[]{:S(2)}) copy-start(s32[1,80]{1,0:T(1,128)} %param.19) | copy-start | bytes 964
  103.8 386.6 %all-gather.14.cloned.1.call-start = ((), (), s32[]{:S(2)}) async-start(), calls=%async_computation.3 | async-start | bytes 15597568 | tf_op jit(solution)/shard_map/all_gather | solution.py:164
  104.4 73.4 %collective-permute-start = (bf16[1280,1280]{1,0:T(8,128)(2,1)}, bf16[1280,1280]{1,0:T(8,128)(2,1)}, u32[]{:S(2)}, u32[]{:S(2)}) collective-permute-start(bf16[1280,1280]{1,0:T(8,128)(2,1)} %param.13), channel_id=1, source_target_pairs={{0,64},{64,128},{128,192},{192,0},{1,65},{65,129},{129,193},{193,1... | collective-permute-start | bytes 9830408 | tf_op jit(solution)/shard_map/ppermute | solution.py:21
  105.2 87.5 %collective-permute-start.1 = (bf16[1280,1280]{1,0:T(8,128)(2,1)}, bf16[1280,1280]{1,0:T(8,128)(2,1)}, u32[]{:S(2)}, u32[]{:S(2)}) collective-permute-start(bf16[1280,1280]{1,0:T(8,128)(2,1)} %param.13), channel_id=1, source_target_pairs={{0,192},{64,0},{128,64},{192,128},{1,193},{65,1},{129,65},{193,129... | collective-permute-start | bytes 9830408 | tf_op jit(solution)/shard_map/ppermute | solution.py:26
  177.8 72.4 %collective-permute-start.2 = (bf16[1280,1280]{1,0:T(8,128)(2,1)}, bf16[1280,1280]{1,0:T(8,128)(2,1)}, u32[]{:S(2)}, u32[]{:S(2)}) collective-permute-start(bf16[1280,1280]{1,0:T(8,128)(2,1)} %collective-permute-done), channel_id=1, source_target_pairs={{0,64},{64,128},{128,192},{192,0},{1,65},{65,129},{129,193},{193,1... | collective-permute-start | bytes 9830408 | tf_op jit(solution)/shard_map/ppermute | solution.py:21
  264.6 4.7 copy-start.1
Sparse Core Ops, SparseCore 0:
  9.8 26.8 all-gather.9
  38.5 59.5 all-gather.7
  104.0 62.9 all-gather.11
  168.6 321.7 all-gather.13
